TPU v7x, 256 devices: a whole 4x4x8 slice. The times are simulated.
256 devices in a mesh: row: 16 (over z, y_hi), col: 16 (over y_lo, x, core).
Axes of the slice: x: 4, y: 4 (y_hi: 2, y_lo: 2; y = y_hi * 2 + y_lo), z: 8, core: 2. Of those that a mesh axis runs over, the one named last changes fastest.
Arguments:
- object_field: float32 [2, 4096, 4096], P(None, 'row', 'col'), may hold values from -5 to 5
- probe: float32 [2, 256, 256], replicated, may hold values from -6 to 6
- amplitudes: float32 [16, 16, 4, 256, 256], P('row', 'col'), may hold values from 0 to 11, as said below
- positions: int32 [16, 16, 4, 2], P('row', 'col'), may hold values from 0 to 64
Outputs:
- object_next: float32 [2, 4096, 4096], P(None, 'row', 'col')
- probe_next: float32 [2, 256, 256], replicated
Inputs may be any that keep to these rules, and one draw needn't show every extreme that they name: Positive amplitudes.
All inputs are finite; a program needn't handle non-finite values.
Results may differ from a plain program's by a relative error of at most 0.0003.
Values sent between devices are 32-bit elements; how exact they have to be, the bound alone decides.
A program may use at most 64 MiB of HBM per device.

v0:
```python
import math
import jax
import jax.numpy as jnp
from jax import lax
from jax.sharding import PartitionSpec as P

W = 256
MARGIN = 32
smoothing = 0.1
regular = 1.0
epsilon = 1e-06


def padded(block, sides, width):
    for axis, dim in sides:
        count = lax.axis_size(axis)
        forward = [(i, i + 1) for i in range(count - 1)]
        backward = [(target, source) for source, target in forward]
        low = lax.ppermute(
            lax.slice_in_dim(block, block.shape[dim] - width, None, axis=dim), axis, forward
        )
        high = lax.ppermute(lax.slice_in_dim(block, 0, width, axis=dim), axis, backward)
        block = jnp.concatenate([low, block, high], axis=dim)
    return block


def shifted(block, axis, distance):
    devices = range(lax.axis_size(axis))
    route = [(i - distance, i) for i in devices if i - distance in devices]
    return lax.ppermute(block, axis, route)


def tables(length):
    indices = jnp.arange(length, dtype=jnp.int32)
    phases = (indices[:, None] * indices[None, :] % length).astype(jnp.float32) * (
        2.0 * math.pi / length
    )
    scaling = 1.0 / math.sqrt(length)
    cosine = jnp.cos(phases) * scaling
    sines = jnp.sin(phases) * scaling
    forward = jnp.concatenate(
        [jnp.concatenate([cosine, sines], 1), jnp.concatenate([-sines, cosine], 1)], 0
    )
    inverse = jnp.concatenate(
        [jnp.concatenate([cosine, -sines], 1), jnp.concatenate([sines, cosine], 1)], 0
    )
    return (forward, inverse)


def transform(wavefield, left_matrix, right_matrix):
    length = wavefield.shape[1]
    stacked = wavefield.reshape(2 * length, length)
    mixed = jnp.dot(left_matrix, stacked, precision=lax.Precision.HIGHEST)
    paired = jnp.concatenate([mixed[:length], mixed[length:]], axis=1)
    result = jnp.dot(paired, right_matrix, precision=lax.Precision.HIGHEST)
    return jnp.stack([result[:, :length], result[:, length:]])


def frame_terms(probe, window, amplitude, forward, inverse):
    exit_real = probe[0] * window[0] - probe[1] * window[1]
    exit_imag = probe[0] * window[1] + probe[1] * window[0]
    wave = jnp.stack([exit_real, exit_imag])
    far_field = transform(wave, forward, inverse)
    factor = amplitude / jnp.sqrt(
        far_field[0] * far_field[0] + far_field[1] * far_field[1] + smoothing
    )
    near_field = transform(far_field * factor[None], inverse, forward)
    difference = near_field - wave
    object_real = probe[0] * difference[0] + probe[1] * difference[1]
    object_imag = probe[0] * difference[1] - probe[1] * difference[0]
    probe_real = window[0] * difference[0] + window[1] * difference[1]
    probe_imag = window[0] * difference[1] - window[1] * difference[0]
    window_power = window[0] * window[0] + window[1] * window[1]
    return (
        jnp.stack([object_real, object_imag]),
        jnp.stack([probe_real, probe_imag, window_power]),
    )


def add_edges(middle, leading, trailing, along, tile_side, margin):
    head_pad = [(0, 0), (0, 0), (0, 0)]
    tail_pad = [(0, 0), (0, 0), (0, 0)]
    head_pad[along] = (0, tile_side - margin)
    tail_pad[along] = (tile_side - margin, 0)
    return middle + jnp.pad(leading, head_pad) + jnp.pad(trailing, tail_pad)


def per_device(object_field, probe, amplitudes, positions):
    forward, inverse = tables(W)
    tile_side = object_field.shape[1]
    margin = MARGIN
    window_side = tile_side + 2 * margin
    extended = padded(object_field, (("row", 1), ("col", 2)), MARGIN)
    power_map = probe[0] * probe[0] + probe[1] * probe[1]
    measured = amplitudes[0, 0]
    offsets = positions[0, 0]
    frame_total = measured.shape[0]
    anchor = jnp.zeros((), jnp.int32)

    def visit(frame_index, carried):
        canvas, probe_acc = carried
        amplitude = measured[frame_index]
        offset = offsets[frame_index]
        window = lax.dynamic_slice(extended, (anchor, offset[0], offset[1]), (2, W, W))
        object_term, probe_term = frame_terms(probe, window, amplitude, forward, inverse)
        update = jnp.concatenate([object_term, power_map[None]], 0)
        current = lax.dynamic_slice(canvas, (anchor, offset[0], offset[1]), (3, W, W))
        canvas = lax.dynamic_update_slice(canvas, current + update, (anchor, offset[0], offset[1]))
        return (canvas, probe_acc + probe_term)

    canvas_start = jnp.zeros((3, window_side, window_side), jnp.float32)
    probe_start = jnp.zeros((3, W, W), jnp.float32)
    canvas, probe_acc = lax.fori_loop(0, frame_total, visit, (canvas_start, probe_start))
    from_above = shifted(canvas[:, window_side - margin :, :], "row", 1)
    from_below = shifted(canvas[:, :margin, :], "row", -1)
    row_folded = add_edges(
        canvas[:, margin : margin + tile_side, :], from_above, from_below, 1, tile_side, margin
    )
    from_before = shifted(row_folded[:, :, window_side - margin :], "col", 1)
    from_after = shifted(row_folded[:, :, :margin], "col", -1)
    folded = add_edges(
        row_folded[:, :, margin : margin + tile_side], from_before, from_after, 2, tile_side, margin
    )
    object_next = object_field + folded[0:2] / (folded[2] + regular)
    local_target = jnp.sum(measured * measured)
    devices = lax.axis_size("row") * lax.axis_size("col")
    frame_count = frame_total * devices
    totals, target_sum = lax.psum((probe_acc, local_target), ("row", "col"))
    stepped = probe + totals[0:2] / (totals[2] + regular)
    probe_power = jnp.sum(stepped * stepped)
    target = target_sum / frame_count
    probe_next = stepped * jnp.sqrt(target / (probe_power + epsilon))
    return (object_next, probe_next)


def solution(mesh):
    return jax.shard_map(
        per_device,
        mesh=mesh,
        in_specs=(
            P(None, "row", "col"),
            P(),
            P("row", "col", None, None, None),
            P("row", "col", None, None),
        ),
        out_specs=(P(None, "row", "col"), P()),
        check_vma=False,
    )
```

profile of v0, /device:TPU:2, one launch (start us, length us, event | category | flops | bytes accessed | tf_op | source)
XLA Modules:
  0.0 516.5 jit_solution(1246306254406606753)
XLA Ops:
  8.2 5.1 collective-permute-start
  15.6 1.8 add_bitcast_fusion
  18.5 2.5 collective-permute-done.1
  21.9 1.9 collective-permute-start.2
  23.8 3.6 collective-permute-start.3
  27.7 2.9 collective-permute-done.2
  30.6 1.8 collective-permute-done.3
  32.3 2.4 pad_maximum_fusion.5
  36.0 107.6 %while.16 = (s32[]{:T(128)}, f32[3,320,320]{2,1,0:T(8,128)}, f32[3,256,256]{2,1,0:T(8,128)}, s32[4,2]{0,1:T(2,128)S(1)}, f32[2,256,256]{2,1,0:T(8,128)S(1)}, /*i...) while((s32[]{:T(128)}, f32[3,320,320]{2,1,0:T(8,128)}, ...), condition=%wide.region_1.2_spmd.clone, body=%wide.region_0.1_spmd.clone.sunk | while | flops 3225354240 | bytes 31064388 | solution.py:113
  41.9 1.9 convolution_bitcast_fusion.4
  45.9 1.9 convolution_bitcast_fusion.5
  51.4 2.9 maximum_add_fusion.3
  54.3 8.7 %dynamic_update_slice.9 = f32[3,320,320]{2,1,0:T(8,128)} dynamic-update-slice(f32[3,320,320]{2,1,0:T(8,128)} %get-tuple-element.377, f32[3,256,256]{2,1,0:T(8,128)S(1)} %get-tuple-element.360, s32[]{:T(128)} %constant.57.clone.1..sunk, s32[]{:T(128)S(6)} %select_n.61, s32[]{:T(128)S(6)} %select_n.62) | dynamic-update-slice | bytes 1572868 | tf_op jit(solution)/shard_map/while/body/eval_jaxpr/dynamic_update_slice | solution.py:108
  68.9 1.9 convolution_bitcast_fusion.4
  73.0 1.9 convolution_bitcast_fusion.5
  78.5 3.2 maximum_add_fusion.3
  81.7 8.5 %dynamic_update_slice.9 = f32[3,320,320]{2,1,0:T(8,128)} dynamic-update-slice(f32[3,320,320]{2,1,0:T(8,128)} %get-tuple-element.377, f32[3,256,256]{2,1,0:T(8,128)S(1)} %get-tuple-element.360, s32[]{:T(128)} %constant.57.clone.1..sunk, s32[]{:T(128)S(6)} %select_n.61, s32[]{:T(128)S(6)} %select_n.62) | dynamic-update-slice | bytes 1572868 | tf_op jit(solution)/shard_map/while/body/eval_jaxpr/dynamic_update_slice | solution.py:108
  96.1 1.9 convolution_bitcast_fusion.4
  100.1 1.9 convolution_bitcast_fusion.5
  105.6 3.2 maximum_add_fusion.3
  108.8 8.5 %dynamic_update_slice.9 = f32[3,320,320]{2,1,0:T(8,128)} dynamic-update-slice(f32[3,320,320]{2,1,0:T(8,128)} %get-tuple-element.377, f32[3,256,256]{2,1,0:T(8,128)S(1)} %get-tuple-element.360, s32[]{:T(128)} %constant.57.clone.1..sunk, s32[]{:T(128)S(6)} %select_n.61, s32[]{:T(128)S(6)} %select_n.62) | dynamic-update-slice | bytes 1572868 | tf_op jit(solution)/shard_map/while/body/eval_jaxpr/dynamic_update_slice | solution.py:108
  123.2 1.9 convolution_bitcast_fusion.4
  127.3 1.9 convolution_bitcast_fusion.5
  132.7 3.2 maximum_add_fusion.3
  135.9 7.6 %dynamic_update_slice.9 = f32[3,320,320]{2,1,0:T(8,128)} dynamic-update-slice(f32[3,320,320]{2,1,0:T(8,128)} %get-tuple-element.377, f32[3,256,256]{2,1,0:T(8,128)S(1)} %get-tuple-element.360, s32[]{:T(128)} %constant.57.clone.1..sunk, s32[]{:T(128)S(6)} %select_n.61, s32[]{:T(128)S(6)} %select_n.62) | dynamic-update-slice | bytes 1572868 | tf_op jit(solution)/shard_map/while/body/eval_jaxpr/dynamic_update_slice | solution.py:108
  144.5 5.3 %collective-permute-start.4 = (f32[3,32,320]{2,1,0:T(8,128)S(1)}, f32[3,32,320]{2,1,0:T(8,128)S(1)}, u32[]{:S(2)}, u32[]{:S(2)}) collective-permute-start(f32[3,32,320]{2,1,0:T(8,128)S(1)} %get-tuple-element.249), channel_id=1, source_target_pairs={{0,16},{16,32},{32,48},{48,64},{64,80},{80,96},{96,112},{112,128},... | collective-permute-start | bytes 368648 | tf_op jit(solution)/shard_map/ppermute | solution.py:30
  152.9 6.3 %collective-permute-done.5 = f32[3,32,320]{2,1,0:T(8,128)S(1)} collective-permute-done((f32[3,32,320]{2,1,0:T(8,128)S(1)}, f32[3,32,320]{2,1,0:T(8,128)S(1)}, u32[]{:S(2)}, u32[]{:S(2)}) %collective-permute-start.5) | collective-permute-done | bytes 122912 | tf_op jit(solution)/shard_map/ppermute | solution.py:30
  160.8 2.6 collective-permute-start.6
  163.4 3.0 collective-permute-start.7
  167.3 81.6 %psum.15 = f32[]{:T(128)} all-reduce(f32[]{:T(128)} %multiply_reduce_fusion), channel_id=1, replica_groups=mesh['row'=16,'col'=16] {'row','col'}, use_global_device_ids=true, to_apply=%region_4.5 | all-reduce | flops 1 | bytes 8 | tf_op jit(solution)/shard_map/psum | solution.py:128
  251.4 253.7 %all-reduce.6.cloned.1.call-done = f32[3,256,256]{2,1,0:T(8,128)} async-done(((f32[3,256,256]{2,1,0:T(8,128)}), f32[3,256,256]{2,1,0:T(8,128)}) %all-reduce.6.cloned.1.call-update) | async-done | bytes 786448 | tf_op jit(solution)/shard_map/psum | solution.py:128
  506.2 1.8 multiply_reduce_fusion.1
  (99 shorter events, 47.8 us)
Async XLA Ops:
  7.2 11.3 %copy-start.3 = (f32[2,256,256]{2,1,0:T(8,128)S(1)}, f32[2,256,256]{2,1,0:T(8,128)}, u32[]{:S(2)}) copy-start(f32[2,256,256]{2,1,0:T(8,128)} %param.6) | copy-start | bytes 1572868
  7.2 498.0 %all-reduce.6.cloned.1.call-start = ((), (), s32[]{:S(2)}) async-start(), calls=%async_computation | async-start | bytes 1572864 | tf_op jit(solution)/shard_map/psum | solution.py:128
  8.2 10.2 %collective-permute-start = (f32[2,32,256]{2,1,0:T(8,128)S(1)}, f32[2,32,256]{2,1,0:T(8,128)S(1)}, u32[]{:S(2)}, u32[]{:S(2)}) collective-permute-start(f32[2,32,256]{2,1,0:T(8,128)S(1)} %get-tuple-element.258), channel_id=1, source_target_pairs={{0,16},{16,32},{32,48},{48,64},{64,80},{80,96},{96,112},{112,128},... | collective-permute-start | bytes 196616 | tf_op jit(solution)/shard_map/ppermute | solution.py:19
  13.3 7.7 %collective-permute-start.1 = (f32[2,32,256]{2,1,0:T(8,128)S(1)}, f32[2,32,256]{2,1,0:T(8,128)S(1)}, u32[]{:S(2)}, u32[]{:S(2)}) collective-permute-start(f32[2,32,256]{2,1,0:T(8,128)S(1)} %get-tuple-element.257), channel_id=1, source_target_pairs={{16,0},{32,16},{48,32},{64,48},{80,64},{96,80},{112,96},{128,112},... | collective-permute-start | bytes 196616 | tf_op jit(solution)/shard_map/ppermute | solution.py:22
  21.9 8.7 %collective-permute-start.2 = (f32[2,320,32]{2,1,0:T(8,128)}, f32[2,320,32]{2,1,0:T(8,128)}, u32[]{:S(2)}, u32[]{:S(2)}) collective-permute-start(f32[2,320,32]{2,1,0:T(8,128)} %get-tuple-element.255), channel_id=1, source_target_pairs={{0,1},{1,2},{2,3},{3,4},{4,5},{5,6},{6,7},{7,8},{8,9},{9,10},{10,1... | collective-permute-start | bytes 245768 | tf_op jit(solution)/shard_map/ppermute | solution.py:19
  23.8 8.5 %collective-permute-start.3 = (f32[2,320,32]{2,1,0:T(8,128)}, f32[2,320,32]{2,1,0:T(8,128)}, u32[]{:S(2)}, u32[]{:S(2)}) collective-permute-start(f32[2,320,32]{2,1,0:T(8,128)} %get-tuple-element.256), channel_id=1, source_target_pairs={{1,0},{2,1},{3,2},{4,3},{5,4},{6,5},{7,6},{8,7},{9,8},{10,9},{11,1... | collective-permute-start | bytes 245768 | tf_op jit(solution)/shard_map/ppermute | solution.py:22
  27.7 8.3 %copy-start = (f32[2,256,256]{2,1,0:T(8,128)S(1)}, f32[2,256,256]{2,1,0:T(8,128)}, u32[]{:S(2)}) copy-start(f32[2,256,256]{2,1,0:T(8,128)} %param.7) | copy-start | bytes 1572868
  27.7 8.3 %copy-start.6 = (s32[1,1,4,2]{2,3,1,0:T(2,128)S(1)}, s32[1,1,4,2]{2,3,1,0:T(2,128)}, u32[]{:S(2)}) copy-start(s32[1,1,4,2]{2,3,1,0:T(2,128)} %param.9) | copy-start | bytes 100
  48.9 1.2 copy-start.1
  76.0 1.2 copy-start.1
  103.1 1.2 copy-start.1
  130.2 1.2 copy-start.1
  144.5 8.4 %collective-permute-start.4 = (f32[3,32,320]{2,1,0:T(8,128)S(1)}, f32[3,32,320]{2,1,0:T(8,128)S(1)}, u32[]{:S(2)}, u32[]{:S(2)}) collective-permute-start(f32[3,32,320]{2,1,0:T(8,128)S(1)} %get-tuple-element.249), channel_id=1, source_target_pairs={{0,16},{16,32},{32,48},{48,64},{64,80},{80,96},{96,112},{112,128},... | collective-permute-start | bytes 368648 | tf_op jit(solution)/shard_map/ppermute | solution.py:30
  149.8 16.5 %copy-start.2 = (f32[4,256,256]{2,1,0:T(8,128)S(1)}, f32[4,256,256]{2,1,0:T(8,128)}, u32[]{:S(2)}) copy-start(f32[4,256,256]{2,1,0:T(8,128)} %get-tuple-element.408) | copy-start | bytes 3145732
  149.8 9.4 %collective-permute-start.5 = (f32[3,32,320]{2,1,0:T(8,128)S(1)}, f32[3,32,320]{2,1,0:T(8,128)S(1)}, u32[]{:S(2)}, u32[]{:S(2)}) collective-permute-start(f32[3,32,320]{2,1,0:T(8,128)S(1)} %get-tuple-element.250), channel_id=1, source_target_pairs={{16,0},{32,16},{48,32},{64,48},{80,64},{96,80},{112,96},{128,112},... | collective-permute-start | bytes 368648 | tf_op jit(solution)/shard_map/ppermute | solution.py:30
  160.8 88.7 %collective-permute-start.6 = (f32[3,256,32]{2,1,0:T(8,128)S(1)}, f32[3,256,32]{2,1,0:T(8,128)S(1)}, u32[]{:S(2)}, u32[]{:S(2)}) collective-permute-start(f32[3,256,32]{2,1,0:T(8,128)S(1)} %get-tuple-element.251), channel_id=1, source_target_pairs={{0,1},{1,2},{2,3},{3,4},{4,5},{5,6},{6,7},{7,8},{8,9},{9,10},{10,1... | collective-permute-start | bytes 294920 | tf_op jit(solution)/shard_map/ppermute | solution.py:30
  163.4 86.2 %collective-permute-start.7 = (f32[3,256,32]{2,1,0:T(8,128)S(1)}, f32[3,256,32]{2,1,0:T(8,128)S(1)}, u32[]{:S(2)}, u32[]{:S(2)}) collective-permute-start(f32[3,256,32]{2,1,0:T(8,128)S(1)} %get-tuple-element.252), channel_id=1, source_target_pairs={{1,0},{2,1},{3,2},{4,3},{5,4},{6,5},{7,6},{8,7},{9,8},{10,9},{11,1... | collective-permute-start | bytes 294920 | tf_op jit(solution)/shard_map/ppermute | solution.py:30
  249.5 1.0 copy-start.4
  505.2 3.6 copy-start.5
Sparse Core Ops, SparseCore 0:
  249.6 255.4 all-reduce.5
where the time goes:
time: 519 us; the launch traced here: 516 us
  waiting for transfers between devices  269 us (52%)
  blocking collectives  81.6 us (16%)
  local copies, waits for them, and re-layouts  45.4 us (9%)
  other arithmetic  41.4 us (8%)
  starting transfers between devices  24.3 us (5%)
  matrix products  23.4 us (5%)
  loops' own time  15.9 us (3%)
  between operations  15.6 us (3%)
    psum x1, waiting for transfers between devices, per_device(): totals, target_sum = lax.psum((probe_acc, local_target), ('row', 'col'))  254 us
    psum x1, blocking collectives, per_device(): totals, target_sum = lax.psum((probe_acc, local_target), ('row', 'col'))  81.6 us
    dynamic_update_slice x4, local copies, waits for them, and re-layouts, visit(): lax.dynamic_update_slice(canvas, current + update, (anchor, offset[0], of...  33.4 us
    another operation x1, loops' own time, per_device(): lax.fori_loop(0, frame_total, visit, (canvas_start, probe_start))  15.9 us
    dot_general x8, matrix products, transform(): mixed = jnp.dot(left_matrix, stacked, precision=lax.Precision.HIGHEST)  14.9 us
    add x4, other arithmetic, visit(): current + update  12.6 us
    ppermute x4, starting transfers between devices, shifted(): return lax.ppermute(block, axis, route)  12.3 us
  transfers between devices with their start and end apart: 9, of which 6 were waited for; matrix products, arithmetic and copies ran while one was open for 1% of the time, Pallas kernels for 0%

commit v1 on v0

--- a/solution.py
+++ b/solution.py
@@ -3,6 +3,7 @@
 import jax.numpy as jnp
 from jax import lax
 from jax.sharding import PartitionSpec as P
+from jax.lax import psum
 
 W = 256
 MARGIN = 32
@@ -125,7 +126,8 @@
     local_target = jnp.sum(measured * measured)
     devices = lax.axis_size("row") * lax.axis_size("col")
     frame_count = frame_total * devices
-    totals, target_sum = lax.psum((probe_acc, local_target), ("row", "col"))
+    match_zone = lambda work_x, axis_tag, device_axis: psum(psum(work_x, axis_tag), device_axis)
+    totals, target_sum = match_zone((probe_acc, local_target), axis_tag="col", device_axis="row")
     stepped = probe + totals[0:2] / (totals[2] + regular)
     probe_power = jnp.sum(stepped * stepped)
     target = target_sum / frame_count

time: 519 us -> 453 us (0.87)
  waiting for transfers between devices: 269 us -> 209 us
  blocking collectives: 81.6 us -> 74.4 us
    psum x1 -> x2, waiting for transfers between devices: 254 us -> 193 us  [the longest x1 106 us: per_device(): psum(work_x, axis_tag)]
    psum x1 -> x2, blocking collectives: 81.6 us -> 74.4 us  [the longest x1 43.6 us: per_device(): psum(psum(work_x, axis_tag), device_axis)]
  transfers between devices with their start and end apart: 9 -> 10, of which waited for: 6 -> 7; matrix products, arithmetic and copies ran while one was open for 1% -> 2% of each run, Pallas kernels for 0% -> 0%
where the time goes in v1:
time: 453 us; the launch traced here: 451 us
  waiting for transfers between devices  209 us (46%)
  blocking collectives  74.4 us (16%)
  local copies, waits for them, and re-layouts  44.8 us (10%)
  other arithmetic  43.5 us (10%)
  starting transfers between devices  24.2 us (5%)
  matrix products  23.4 us (5%)
  loops' own time  15.9 us (4%)
  between operations  15.6 us (3%)
    psum x1, waiting for transfers between devices, per_device(): psum(work_x, axis_tag)  106 us
    psum x1, waiting for transfers between devices, per_device(): psum(psum(work_x, axis_tag), device_axis)  87.8 us
    psum x1, blocking collectives, per_device(): psum(psum(work_x, axis_tag), device_axis)  43.6 us
    dynamic_update_slice x4, local copies, waits for them, and re-layouts, visit(): lax.dynamic_update_slice(canvas, current + update, (anchor, offset[0], of...  33.4 us
    psum x1, blocking collectives, per_device(): psum(work_x, axis_tag)  30.8 us
    another operation x1, loops' own time, per_device(): lax.fori_loop(0, frame_total, visit, (canvas_start, probe_start))  15.9 us
    dot_general x8, matrix products, transform(): mixed = jnp.dot(left_matrix, stacked, precision=lax.Precision.HIGHEST)  14.9 us
    add x4, other arithmetic, visit(): current + update  12.5 us
  transfers between devices with their start and end apart: 10, of which 7 were waited for; matrix products, arithmetic and copies ran while one was open for 2% of the time, Pallas kernels for 0%

profile of v1, /device:TPU:2, one launch (start us, length us, event | category | flops | bytes accessed | tf_op | source)
XLA Modules:
  0.0 450.6 jit_solution(6508113162330521939)
XLA Ops:
  8.2 5.1 %collective-permute-start = (f32[2,32,256]{2,1,0:T(8,128)S(1)}, f32[2,32,256]{2,1,0:T(8,128)S(1)}, u32[]{:S(2)}, u32[]{:S(2)}) collective-permute-start(f32[2,32,256]{2,1,0:T(8,128)S(1)} %get-tuple-element.258), channel_id=1, source_target_pairs={{0,16},{16,32},{32,48},{48,64},{64,80},{80,96},{96,112},{112,128},... | collective-permute-start | bytes 196616 | tf_op jit(solution)/shard_map/ppermute | solution.py:20
  18.4 2.5 collective-permute-done.1
  21.9 1.9 collective-permute-start.2
  23.8 3.6 collective-permute-start.3
  27.7 2.9 collective-permute-done.2
  32.3 2.4 pad_maximum_fusion.5
  36.0 107.5 %while.16 = (s32[]{:T(128)}, f32[3,320,320]{2,1,0:T(8,128)}, f32[3,256,256]{2,1,0:T(8,128)}, s32[4,2]{0,1:T(2,128)S(1)}, f32[2,256,256]{2,1,0:T(8,128)S(1)}, /*i...) while((s32[]{:T(128)}, f32[3,320,320]{2,1,0:T(8,128)}, ...), condition=%wide.region_1.2_spmd.clone, body=%wide.region_0.1_spmd.clone.sunk | while | flops 3225354240 | bytes 31064388 | solution.py:114
  41.8 1.9 convolution_bitcast_fusion.4
  45.9 1.9 convolution_bitcast_fusion.5
  51.4 2.9 maximum_add_fusion.3
  54.3 8.8 %dynamic_update_slice.9 = f32[3,320,320]{2,1,0:T(8,128)} dynamic-update-slice(f32[3,320,320]{2,1,0:T(8,128)} %get-tuple-element.377, f32[3,256,256]{2,1,0:T(8,128)S(1)} %get-tuple-element.360, s32[]{:T(128)} %constant.57.clone.1..sunk, s32[]{:T(128)S(6)} %select_n.61, s32[]{:T(128)S(6)} %select_n.62) | dynamic-update-slice | bytes 1572868 | tf_op jit(solution)/shard_map/while/body/eval_jaxpr/dynamic_update_slice | solution.py:109
  68.9 1.9 convolution_bitcast_fusion.4
  73.0 1.9 convolution_bitcast_fusion.5
  78.4 3.2 maximum_add_fusion.3
  81.6 8.5 %dynamic_update_slice.9 = f32[3,320,320]{2,1,0:T(8,128)} dynamic-update-slice(f32[3,320,320]{2,1,0:T(8,128)} %get-tuple-element.377, f32[3,256,256]{2,1,0:T(8,128)S(1)} %get-tuple-element.360, s32[]{:T(128)} %constant.57.clone.1..sunk, s32[]{:T(128)S(6)} %select_n.61, s32[]{:T(128)S(6)} %select_n.62) | dynamic-update-slice | bytes 1572868 | tf_op jit(solution)/shard_map/while/body/eval_jaxpr/dynamic_update_slice | solution.py:109
  96.0 1.9 convolution_bitcast_fusion.4
  100.1 1.9 convolution_bitcast_fusion.5
  105.5 3.2 maximum_add_fusion.3
  108.7 8.5 %dynamic_update_slice.9 = f32[3,320,320]{2,1,0:T(8,128)} dynamic-update-slice(f32[3,320,320]{2,1,0:T(8,128)} %get-tuple-element.377, f32[3,256,256]{2,1,0:T(8,128)S(1)} %get-tuple-element.360, s32[]{:T(128)} %constant.57.clone.1..sunk, s32[]{:T(128)S(6)} %select_n.61, s32[]{:T(128)S(6)} %select_n.62) | dynamic-update-slice | bytes 1572868 | tf_op jit(solution)/shard_map/while/body/eval_jaxpr/dynamic_update_slice | solution.py:109
  123.1 1.9 convolution_bitcast_fusion.4
  127.2 1.9 convolution_bitcast_fusion.5
  132.7 3.2 maximum_add_fusion.3
  135.8 7.6 %dynamic_update_slice.9 = f32[3,320,320]{2,1,0:T(8,128)} dynamic-update-slice(f32[3,320,320]{2,1,0:T(8,128)} %get-tuple-element.377, f32[3,256,256]{2,1,0:T(8,128)S(1)} %get-tuple-element.360, s32[]{:T(128)} %constant.57.clone.1..sunk, s32[]{:T(128)S(6)} %select_n.61, s32[]{:T(128)S(6)} %select_n.62) | dynamic-update-slice | bytes 1572868 | tf_op jit(solution)/shard_map/while/body/eval_jaxpr/dynamic_update_slice | solution.py:109
  144.5 5.3 %collective-permute-start.4 = (f32[3,32,320]{2,1,0:T(8,128)S(1)}, f32[3,32,320]{2,1,0:T(8,128)S(1)}, u32[]{:S(2)}, u32[]{:S(2)}) collective-permute-start(f32[3,32,320]{2,1,0:T(8,128)S(1)} %get-tuple-element.249), channel_id=1, source_target_pairs={{0,16},{16,32},{32,48},{48,64},{64,80},{80,96},{96,112},{112,128},... | collective-permute-start | bytes 368648 | tf_op jit(solution)/shard_map/ppermute | solution.py:31
  153.0 6.2 %collective-permute-done.5 = f32[3,32,320]{2,1,0:T(8,128)S(1)} collective-permute-done((f32[3,32,320]{2,1,0:T(8,128)S(1)}, f32[3,32,320]{2,1,0:T(8,128)S(1)}, u32[]{:S(2)}, u32[]{:S(2)}) %collective-permute-start.5) | collective-permute-done | bytes 122912 | tf_op jit(solution)/shard_map/ppermute | solution.py:31
  160.7 2.5 collective-permute-start.6
  163.3 3.0 collective-permute-start.7
  166.3 105.7 %all-reduce.7.cloned.1.call-done = f32[3,256,256]{2,1,0:T(8,128)} async-done(((f32[3,256,256]{2,1,0:T(8,128)}), f32[3,256,256]{2,1,0:T(8,128)}) %all-reduce.7.cloned.1.call-update) | async-done | bytes 786448 | tf_op jit(solution)/shard_map/psum | solution.py:129
  272.0 2.1 multiply_reduce_fusion
  274.1 30.8 %psum.30 = f32[]{:T(128)} all-reduce(f32[]{:T(128)} %multiply_reduce_fusion), channel_id=1, replica_groups=mesh['row'=16,'col'=16] {'col'}, use_global_device_ids=true, to_apply=%region_5.6 | all-reduce | flops 1 | bytes 8 | tf_op jit(solution)/shard_map/psum | solution.py:129
  305.0 43.6 %psum.31 = f32[]{:T(128)} all-reduce(f32[]{:T(128)} %psum.30), channel_id=1, replica_groups=mesh['row'=16,'col'=16] {'row'}, use_global_device_ids=true, to_apply=%region_6.7 | all-reduce | flops 1 | bytes 8 | tf_op jit(solution)/shard_map/psum | solution.py:129
  351.5 87.8 %all-reduce.9.cloned.1.call-done = f32[3,256,256]{2,1,0:T(8,128)} async-done(((f32[3,256,256]{2,1,0:T(8,128)}), f32[3,256,256]{2,1,0:T(8,128)}) %all-reduce.9.cloned.1.call-update) | async-done | bytes 786448 | tf_op jit(solution)/shard_map/psum | solution.py:129
  (101 shorter events, 52.7 us)
Async XLA Ops:
  7.2 11.2 %copy-start.2 = (f32[2,256,256]{2,1,0:T(8,128)S(1)}, f32[2,256,256]{2,1,0:T(8,128)}, u32[]{:S(2)}) copy-start(f32[2,256,256]{2,1,0:T(8,128)} %param.6) | copy-start | bytes 1572868
  7.2 264.8 %all-reduce.7.cloned.1.call-start = ((), (), s32[]{:S(2)}) async-start(), calls=%async_computation | async-start | bytes 1572864 | tf_op jit(solution)/shard_map/psum | solution.py:129
  8.2 10.2 %collective-permute-start = (f32[2,32,256]{2,1,0:T(8,128)S(1)}, f32[2,32,256]{2,1,0:T(8,128)S(1)}, u32[]{:S(2)}, u32[]{:S(2)}) collective-permute-start(f32[2,32,256]{2,1,0:T(8,128)S(1)} %get-tuple-element.258), channel_id=1, source_target_pairs={{0,16},{16,32},{32,48},{48,64},{64,80},{80,96},{96,112},{112,128},... | collective-permute-start | bytes 196616 | tf_op jit(solution)/shard_map/ppermute | solution.py:20
  13.3 7.7 %collective-permute-start.1 = (f32[2,32,256]{2,1,0:T(8,128)S(1)}, f32[2,32,256]{2,1,0:T(8,128)S(1)}, u32[]{:S(2)}, u32[]{:S(2)}) collective-permute-start(f32[2,32,256]{2,1,0:T(8,128)S(1)} %get-tuple-element.257), channel_id=1, source_target_pairs={{16,0},{32,16},{48,32},{64,48},{80,64},{96,80},{112,96},{128,112},... | collective-permute-start | bytes 196616 | tf_op jit(solution)/shard_map/ppermute | solution.py:23
  21.9 8.7 %collective-permute-start.2 = (f32[2,320,32]{2,1,0:T(8,128)}, f32[2,320,32]{2,1,0:T(8,128)}, u32[]{:S(2)}, u32[]{:S(2)}) collective-permute-start(f32[2,320,32]{2,1,0:T(8,128)} %get-tuple-element.255), channel_id=1, source_target_pairs={{0,1},{1,2},{2,3},{3,4},{4,5},{5,6},{6,7},{7,8},{8,9},{9,10},{10,1... | collective-permute-start | bytes 245768 | tf_op jit(solution)/shard_map/ppermute | solution.py:20
  23.8 8.5 %collective-permute-start.3 = (f32[2,320,32]{2,1,0:T(8,128)}, f32[2,320,32]{2,1,0:T(8,128)}, u32[]{:S(2)}, u32[]{:S(2)}) collective-permute-start(f32[2,320,32]{2,1,0:T(8,128)} %get-tuple-element.256), channel_id=1, source_target_pairs={{1,0},{2,1},{3,2},{4,3},{5,4},{6,5},{7,6},{8,7},{9,8},{10,9},{11,1... | collective-permute-start | bytes 245768 | tf_op jit(solution)/shard_map/ppermute | solution.py:23
  27.7 8.3 %copy-start = (f32[2,256,256]{2,1,0:T(8,128)S(1)}, f32[2,256,256]{2,1,0:T(8,128)}, u32[]{:S(2)}) copy-start(f32[2,256,256]{2,1,0:T(8,128)} %param.7) | copy-start | bytes 1572868
  27.7 8.3 %copy-start.5 = (s32[1,1,4,2]{2,3,1,0:T(2,128)S(1)}, s32[1,1,4,2]{2,3,1,0:T(2,128)}, u32[]{:S(2)}) copy-start(s32[1,1,4,2]{2,3,1,0:T(2,128)} %param.9) | copy-start | bytes 100
  48.9 1.2 copy-start.1
  76.0 1.2 copy-start.1
  103.1 1.2 copy-start.1
  130.2 1.2 copy-start.1
  143.5 295.8 %all-reduce.9.cloned.1.call-start = ((), (), s32[]{:S(2)}) async-start(), calls=%async_computation.1 | async-start | bytes 1572864 | tf_op jit(solution)/shard_map/psum | solution.py:129
  144.5 8.5 %collective-permute-start.4 = (f32[3,32,320]{2,1,0:T(8,128)S(1)}, f32[3,32,320]{2,1,0:T(8,128)S(1)}, u32[]{:S(2)}, u32[]{:S(2)}) collective-permute-start(f32[3,32,320]{2,1,0:T(8,128)S(1)} %get-tuple-element.249), channel_id=1, source_target_pairs={{0,16},{16,32},{32,48},{48,64},{64,80},{80,96},{96,112},{112,128},... | collective-permute-start | bytes 368648 | tf_op jit(solution)/shard_map/ppermute | solution.py:31
  149.9 9.3 %collective-permute-start.5 = (f32[3,32,320]{2,1,0:T(8,128)S(1)}, f32[3,32,320]{2,1,0:T(8,128)S(1)}, u32[]{:S(2)}, u32[]{:S(2)}) collective-permute-start(f32[3,32,320]{2,1,0:T(8,128)S(1)} %get-tuple-element.250), channel_id=1, source_target_pairs={{16,0},{32,16},{48,32},{64,48},{80,64},{96,80},{112,96},{128,112},... | collective-permute-start | bytes 368648 | tf_op jit(solution)/shard_map/ppermute | solution.py:31
  160.7 188.5 %collective-permute-start.6 = (f32[3,256,32]{2,1,0:T(8,128)S(1)}, f32[3,256,32]{2,1,0:T(8,128)S(1)}, u32[]{:S(2)}, u32[]{:S(2)}) collective-permute-start(f32[3,256,32]{2,1,0:T(8,128)S(1)} %get-tuple-element.251), channel_id=1, source_target_pairs={{0,1},{1,2},{2,3},{3,4},{4,5},{5,6},{6,7},{7,8},{8,9},{9,10},{10,1... | collective-permute-start | bytes 294920 | tf_op jit(solution)/shard_map/ppermute | solution.py:31
  163.3 185.9 %collective-permute-start.7 = (f32[3,256,32]{2,1,0:T(8,128)S(1)}, f32[3,256,32]{2,1,0:T(8,128)}, u32[]{:S(2)}, u32[]{:S(2)}) collective-permute-start(f32[3,256,32]{2,1,0:T(8,128)S(1)} %get-tuple-element.252), channel_id=1, source_target_pairs={{1,0},{2,1},{3,2},{4,3},{5,4},{6,5},{7,6},{8,7},{9,8},{10,9},{11,1... | collective-permute-start | bytes 294920 | tf_op jit(solution)/shard_map/ppermute | solution.py:31
  274.1 76.5 %copy-start.3 = (f32[2,256,256]{2,1,0:T(8,128)S(1)}, f32[2,256,256]{2,1,0:T(8,128)}, u32[]{:S(2)}) copy-start(f32[2,256,256]{2,1,0:T(8,128)} %param.6) | copy-start | bytes 1572868
  439.3 3.6 copy-start.4
Sparse Core Ops, SparseCore 0:
  143.6 128.3 all-reduce.6
  274.6 164.6 all-reduce.8
